TPU v7x, 512 devices: a whole 4x8x8 slice. The times are simulated.
512 devices in a mesh: context: 32 (over y, x), tensor: 4 (over z_hi), dp: 4 (over z_lo, core).
Axes of the slice: x: 4, y: 8, z: 8 (z_hi: 4, z_lo: 2; z = z_hi * 2 + z_lo), core: 2. Of those that a mesh axis runs over, the one named last changes fastest.
Arguments:
- grad_out: bfloat16 [4, 8192, 1024], P('dp', 'context', 'tensor'), may hold values from -6 to 6
- inputs: bfloat16 [4, 8192, 1024], P('dp', 'context', 'tensor'), may hold values from -0.03125 to 0.03125
- filt: bfloat16 [8192, 1024], P('context', 'tensor'), may hold values from -0.0625 to 0.0625
Outputs:
- input_grad: bfloat16 [4, 8192, 1024], P('dp', 'context', 'tensor')
- filter_grad: float32 [8192, 1024], P('context', 'tensor')
All inputs are finite; a program needn't handle non-finite values.
Results may differ from a plain program's by a relative error of at most 0.001.
Values may be sent and summed in bfloat16 or wider, within the bound.
No kernel may reach another device: no remote copies, remote signals or barrier semaphores. Data moves between devices by JAX's collectives and lax.ppermute only.
A program may use at most 64 MiB of HBM per device.

v0:
```python
import functools
import jax
import jax.numpy as jnp
from jax import lax
from jax.experimental import pallas as pl
from jax.experimental.pallas import tpu as pltpu
from jax.sharding import PartitionSpec as P

F32 = jnp.float32
BF16 = jnp.bfloat16


def nt_dot(left, right):
    return lax.dot_general(left, right, (((1,), (1,)), ((), ())), preferred_element_type=F32)


def spread_row(ref, row, lane):
    return ref[pl.ds(2 * lane + row, 8, stride=0), :]


def build_lags(rows, out_ref):
    sub = lax.broadcasted_iota(jnp.int32, (8, 128), 0)
    lane = lax.broadcasted_iota(jnp.int32, (8, 128), 1)
    masks = [lane < sub + 8 * s for s in range(4)]
    before = [jnp.zeros((8, 128), F32) for _ in range(4)]
    for d in range(32):
        low, high = rows(d)
        pieces = []
        for s in range(4):
            low_turned = pltpu.roll(low, 8 * s, 1, stride=1, stride_axis=0)
            high_turned = pltpu.roll(high, 8 * s, 1, stride=1, stride_axis=0)
            pieces.append(
                jnp.concatenate(
                    [
                        jnp.where(masks[s], before[s], low_turned),
                        jnp.where(masks[s], low_turned, high_turned),
                    ],
                    axis=1,
                )
            )
            before[s] = high_turned
        out_ref[32 * d : 32 * d + 32, :] = jnp.concatenate(pieces, axis=0).astype(BF16)


def build_windows(rows, out_ref):
    sub = lax.broadcasted_iota(jnp.int32, (8, 128), 0)
    lane = lax.broadcasted_iota(jnp.int32, (8, 128), 1)
    shift = 7 - sub
    inside = lane < 128 - 32 * lax.rem(shift, 4)
    early = shift < 4

    def turned(a):
        once = [pltpu.roll(half, 16, 1, stride=16, stride_axis=0) for half in rows(a)]
        return [pltpu.roll(half, 16, 1, stride=16, stride_axis=0) for half in once]

    here = turned(0)
    pair = []
    for a in range(32):
        after = turned(a + 1) if a < 31 else [jnp.zeros((8, 128), F32)] * 2
        first = jnp.where(inside, here[0], here[1])
        second = jnp.where(inside, here[1], after[0])
        third = jnp.where(inside, after[0], after[1])
        pair.append(
            jnp.concatenate(
                [jnp.where(early, first, second), jnp.where(early, second, third)], axis=1
            )
        )
        if a % 2 == 1:
            out_ref[8 * a - 8 : 8 * a + 8, :] = jnp.concatenate(pair, axis=0).astype(BF16)
            pair = []
        here = after


def add_products(window_ref, lag_ref, total_ref):
    for q in range(4):
        part = nt_dot(window_ref[64 * q :, :], lag_ref[256 * q : 256 * q + 256, :])
        size = 256 - 64 * q
        total_ref[0:size, :] += part[:, 0:128]
        total_ref[0 : size - 32, :] += part[32:, 128:256]


def finish(total_ref, flat_ref):
    lane = lax.broadcasted_iota(jnp.int32, (256, 128), 1)
    sub = lax.broadcasted_iota(jnp.int32, (256, 128), 0)
    group = lane // 32
    mixed = total_ref[0:256, :]
    for p in range(1, 4):
        mixed = jnp.where(group == p, total_ref[8 * p : 8 * p + 256, :], mixed)
    mixed = mixed + pltpu.roll(mixed, 64, 1)
    mixed = mixed + pltpu.roll(mixed, 32, 1)
    flat_ref[...] = jnp.where(group == 3 - lax.rem(sub, 4), mixed, 0.0)

    def gathered(first):
        return sum(flat_ref[pl.ds(7 - r, 32, stride=8), :] for r in range(first, first + 4))

    return gathered(0), gathered(4)


def conv_kernel(r_ref, dx_ref, dh_ref, lag_f, lag_x, window, total_dx, total_dh, flat):
    def channel(c, carry):
        def filter_rows(d):
            return (spread_row(r_ref, d * 8 + c, 512), spread_row(r_ref, d * 8 + 4 + c, 512))

        build_lags(filter_rows, lag_f)
        total_dh[...] = jnp.zeros_like(total_dh)

        def batch(b, inner):
            def rows_at(offset):
                def rows(d):
                    row = d * 8 + b * 2 + c
                    return (spread_row(r_ref, row, offset), spread_row(r_ref, row, offset + 128))

                return rows

            build_windows(rows_at(0), window)
            build_lags(rows_at(256), lag_x)
            total_dx[...] = jnp.zeros_like(total_dx)
            add_products(window, lag_f, total_dx)
            add_products(window, lag_x, total_dh)
            low, high = finish(total_dx, flat)
            dx_ref[pl.ds(b * 2 + c, 32, stride=8), :] = low
            dx_ref[pl.ds(256 + b * 2 + c, 32, stride=8), :] = high
            return inner

        lax.fori_loop(0, 4, batch, 0)
        low, high = finish(total_dh, flat)
        dh_ref[pl.ds(c, 32, stride=2), :] = low
        dh_ref[pl.ds(64 + c, 32, stride=2), :] = high
        return carry

    lax.fori_loop(0, 2, channel, 0)


def conv_call(r):
    vmem = pl.BlockSpec(memory_space=pltpu.VMEM)
    return pl.pallas_call(
        conv_kernel,
        out_shape=(
            jax.ShapeDtypeStruct((512, 128), F32),
            jax.ShapeDtypeStruct((128, 128), F32),
        ),
        in_specs=[vmem],
        out_specs=(vmem, vmem),
        scratch_shapes=[
            pltpu.VMEM((1024, 256), BF16),
            pltpu.VMEM((1024, 256), BF16),
            pltpu.VMEM((256, 256), BF16),
            pltpu.VMEM((280, 128), F32),
            pltpu.VMEM((280, 128), F32),
            pltpu.VMEM((256, 128), F32),
        ],
    )(r)


def body(grad_out, inputs, filt):
    turn = lax.axis_index("dp")
    wide = grad_out.shape[2]
    filter_turned = filt.T
    piece = lax.dynamic_slice(filter_turned, (0, 128 * (turn // 2)), (wide, 128))
    packed = jnp.concatenate([grad_out[0].T, inputs[0].T, piece], axis=1).reshape(128, 2, 640)
    arrived = lax.all_to_all(packed, ("context", "dp"), 0, 0, tiled=True)
    lanes = arrived.astype(F32).reshape(256, 5, 128).transpose(1, 0, 2).reshape(1280, 128)
    dx, dh = conv_call(lanes)
    dx = dx.reshape(2, 128, 2, 128).transpose(1, 2, 0, 3).reshape(128, 2, 256)
    dh = dh.reshape(2, 32, 2, 128).transpose(1, 2, 0, 3).reshape(32, 1, 2, 256)
    dh = jnp.broadcast_to(dh, (32, 4, 2, 256)).reshape(128, 2, 256)
    upper = lax.reduce_precision(dh, 8, 7)
    lower = (dh - upper).astype(BF16)
    outgoing = jnp.concatenate([dx.astype(BF16), upper.astype(BF16), lower], axis=2)
    returned = lax.all_to_all(outgoing, ("context", "dp"), 0, 0, tiled=True).reshape(256, 768)
    input_grad = returned[:, 0:256].T
    filter_grad = returned[:, 256:512].astype(F32) + returned[:, 512:768].astype(F32)
    return input_grad[None], filter_grad.T


def solution(mesh):
    return jax.shard_map(
        body,
        mesh=mesh,
        in_specs=(
            P("dp", "context", "tensor"),
            P("dp", "context", "tensor"),
            P("context", "tensor"),
        ),
        out_specs=(P("dp", "context", "tensor"), P("context", "tensor")),
        check_vma=False,
    )
```

profile of v0, /device:TPU:1, one launch (start us, length us, event | category | flops | bytes accessed | tf_op | source)
XLA Modules:
  0.0 67.9 jit_solution(15685904624034182280)
XLA Ops:
  0.6 0.0 copy-start
  0.6 0.0 copy-start.1
  0.7 0.9 %copy-done = bf16[256,256]{1,0:T(8,128)(2,1)S(1)} copy-done((bf16[256,256]{1,0:T(8,128)(2,1)S(1)}, bf16[256,256]{1,0:T(8,128)(2,1)}, u32[]{:S(2)}) %copy-start) | copy-done | bytes 131096
  1.5 0.1 copy-done.1
  1.6 0.9 %pad_maximum_fusion.1 = bf16[256,640]{0,1:T(8,128)(2,1)S(1)} fusion(bf16[256,128]{0,1:T(8,128)(2,1)S(1)} %dynamic-slice_bitcast_fusion, bf16[256,256]{0,1:T(8,128)(2,1)S(1)} %bitcast.33, bf16[256,256]{0,1:T(8,128)(2,1)} %bitcast.34), kind=kLoop, calls=%fused_computation.3 | loop fusion | flops 983040 | bytes 655360 | tf_op jit(solution)/shard_map/concatenate | solution.py:160
  2.5 0.2 copy.23
  2.7 0.1 reshape.31
  2.9 28.8 %all_to_all.10 = bf16[128,2,640]{2,1,0:T(2,128)(2,1)S(1)} all-to-all(bf16[128,2,640]{2,1,0:T(2,128)(2,1)S(1)} %reshape.31), channel_id=1, replica_groups=mesh['context'=32,'tensor'=4,'dp'=4] {'context','dp'}, dimensions={0} | all-to-all | bytes 655360 | tf_op jit(solution)/shard_map/all_to_all | solution.py:161
  31.7 0.2 reshape.42
  31.8 1.0 %copy.24 = f32[5,256,128]{2,1,0:T(8,128)} copy(f32[5,256,128]{2,0,1:T(8,128)S(1)} %bitcast.27) | data formatting | bytes 1310720 | tf_op jit(solution)/shard_map/reshape | solution.py:162
  32.8 7.9 %shard_map.50 = (f32[512,128]{1,0:T(8,128)}, f32[128,128]{1,0:T(8,128)}) custom-call(f32[1280,128]{1,0:T(8,128)} %bitcast.28), custom_call_target="tpu_custom_call" | custom-call | tf_op jit(solution)/shard_map/pallas_call | solution.py:136
  40.8 1.0 %convert_element_type.25 = bf16[512,128]{1,0:T(8,128)(2,1)S(1)} convert(f32[512,128]{1,0:T(8,128)} %get-tuple-element.4) | non-fusion elementwise | flops 65536 | bytes 393216 | tf_op jit(solution)/shard_map/convert_element_type | solution.py:169
  41.7 0.0 copy-start.2
  41.7 0.1 copy.25
  41.9 0.7 %copy-done.2 = f32[128,128]{1,0:T(8,128)S(1)} copy-done((f32[128,128]{1,0:T(8,128)S(1)}, f32[128,128]{1,0:T(8,128)}, u32[]{:S(2)}) %copy-start.2) | copy-done | bytes 65560
  42.6 0.1 copy.34
  42.6 0.1 broadcast_in_dim.10
  42.7 0.1 copy.27
  42.7 0.1 broadcast_in_dim.11
  42.8 0.1 copy.28
  43.0 0.4 copy.30
  43.5 22.6 %all_to_all.11 = bf16[128,2,768]{2,1,0:T(2,128)(2,1)S(1)} all-to-all(bf16[128,2,768]{2,1,0:T(2,128)(2,1)S(1)} %copy.30), channel_id=1, replica_groups=mesh['context'=32,'tensor'=4,'dp'=4] {'context','dp'}, dimensions={0} | all-to-all | bytes 786432 | tf_op jit(solution)/shard_map/all_to_all | solution.py:170
  66.1 0.1 reshape.37
  66.3 0.8 %copy.32 = f32[256,256]{1,0:T(8,128)} copy(f32[256,256]{0,1:T(8,128)S(1)} %add_bitcast_fusion) | data formatting | bytes 524288
  67.2 0.8 %copy.31 = bf16[1,256,256]{2,1,0:T(8,128)(2,1)} copy(bf16[1,256,256]{1,2,0:T(8,128)(2,1)S(1)} %slice_bitcast_fusion) | data formatting | bytes 262144
  (5 shorter events, 0.1 us)
Async XLA Ops:
  0.6 0.9 %copy-start = (bf16[256,256]{1,0:T(8,128)(2,1)S(1)}, bf16[256,256]{1,0:T(8,128)(2,1)}, u32[]{:S(2)}) copy-start(bf16[256,256]{1,0:T(8,128)(2,1)} %param.5) | copy-start | bytes 393220
  0.6 1.0 %copy-start.1 = (bf16[1,256,256]{2,1,0:T(8,128)(2,1)S(1)}, bf16[1,256,256]{2,1,0:T(8,128)(2,1)}, u32[]{:S(2)}) copy-start(bf16[1,256,256]{2,1,0:T(8,128)(2,1)} %param.4) | copy-start | bytes 393220
  41.7 0.8 %copy-start.2 = (f32[128,128]{1,0:T(8,128)S(1)}, f32[128,128]{1,0:T(8,128)}, u32[]{:S(2)}) copy-start(f32[128,128]{1,0:T(8,128)} %get-tuple-element.5) | copy-start | bytes 196612
where the time goes:
time: 68.9 us; the launch traced here: 67.9 us
  blocking collectives  51.4 us (75%)
  Pallas kernels  7.94 us (12%)
  local copies, waits for them, and re-layouts  5.8 us (8%)
  other arithmetic  1.99 us (3%)
  between operations  0.78 us (1%)
    all_to_all x1, blocking collectives, body(): arrived = lax.all_to_all(packed, ('context', 'dp'), 0, 0, tiled=True)  28.8 us
    all_to_all x1, blocking collectives, body(): lax.all_to_all(outgoing, ('context', 'dp'), 0, 0, tiled=True)  22.6 us
    pallas_call x1, Pallas kernels, conv_call(): pl.pallas_call(conv_kernel, out_shape=(jax.ShapeDtypeStruct((512, 128), F...  7.94 us
    unnamed x8, local copies, waits for them, and re-layouts  3.23 us

commit v1 on v0

--- a/solution.py
+++ b/solution.py
@@ -149,6 +149,7 @@
             pltpu.VMEM((280, 128), F32),
             pltpu.VMEM((256, 128), F32),
         ],
+        compiler_params=pltpu.CompilerParams(vmem_limit_bytes=6 * 1024 * 1024),
     )(r)
 
 

time: 68.9 us -> 64.6 us (0.938)
  Pallas kernels: 7.94 us -> 6.21 us
  local copies, waits for them, and re-layouts: 5.8 us -> 4.27 us
  other arithmetic: 1.99 us -> 1.04 us
    pallas_call x1, Pallas kernels: 7.94 us -> 6.21 us  [conv_call(): pl.pallas_call(conv_kernel, out_shape=(jax.ShapeDtypeStruct((512, 128), F...]
    convert_element_type x1, other arithmetic: 0.96 us -> 0.02 us  [body(): dx.astype(BF16)]
    reshape x2, local copies, waits for them, and re-layouts: 1.14 us -> 0.31 us  [body(): arrived.astype(F32).reshape(256, 5, 128).transpose(1, 0, 2)]
    unnamed x8 -> x6, local copies, waits for them, and re-layouts: 3.23 us -> 2.53 us
where the time goes in v1:
time: 64.6 us; the launch traced here: 63.7 us
  blocking collectives  51.4 us (80%)
  Pallas kernels  6.21 us (10%)
  local copies, waits for them, and re-layouts  4.27 us (7%)
  other arithmetic  1.04 us (2%)
  between operations  0.79 us (1%)
    all_to_all x1, blocking collectives, body(): arrived = lax.all_to_all(packed, ('context', 'dp'), 0, 0, tiled=True)  28.8 us
    all_to_all x1, blocking collectives, body(): lax.all_to_all(outgoing, ('context', 'dp'), 0, 0, tiled=True)  22.6 us
    pallas_call x1, Pallas kernels, conv_call(): pl.pallas_call(conv_kernel, out_shape=(jax.ShapeDtypeStruct((512, 128), F...  6.21 us
    unnamed x6, local copies, waits for them, and re-layouts  2.53 us

profile of v1, /device:TPU:1, one launch (start us, length us, event | category | flops | bytes accessed | tf_op | source)
XLA Modules:
  0.0 63.7 jit_solution(4663552978547884977)
XLA Ops:
  0.6 0.0 copy-start
  0.6 0.0 copy-start.1
  0.7 0.9 %copy-done = bf16[256,256]{1,0:T(8,128)(2,1)S(1)} copy-done((bf16[256,256]{1,0:T(8,128)(2,1)S(1)}, bf16[256,256]{1,0:T(8,128)(2,1)}, u32[]{:S(2)}) %copy-start) | copy-done | bytes 131096
  1.5 0.1 copy-done.1
  1.6 0.9 %pad_maximum_fusion.1 = bf16[256,640]{0,1:T(8,128)(2,1)S(1)} fusion(bf16[256,128]{0,1:T(8,128)(2,1)S(1)} %dynamic-slice_bitcast_fusion, bf16[256,256]{0,1:T(8,128)(2,1)S(1)} %bitcast.34, bf16[256,256]{0,1:T(8,128)(2,1)} %bitcast.35), kind=kLoop, calls=%fused_computation.3 | loop fusion | flops 983040 | bytes 655360 | tf_op jit(solution)/shard_map/concatenate | solution.py:161
  2.5 0.2 copy.23
  2.7 0.1 reshape.31
  2.9 28.8 %all_to_all.10 = bf16[128,2,640]{2,1,0:T(2,128)(2,1)S(1)} all-to-all(bf16[128,2,640]{2,1,0:T(2,128)(2,1)S(1)} %reshape.31), channel_id=1, replica_groups=mesh['context'=32,'tensor'=4,'dp'=4] {'context','dp'}, dimensions={0} | all-to-all | bytes 655360 | tf_op jit(solution)/shard_map/all_to_all | solution.py:162
  31.7 0.2 reshape.42
  31.8 0.1 copy.24
  32.0 6.2 %shard_map.50 = (f32[512,128]{1,0:T(8,128)S(1)}, f32[128,128]{1,0:T(8,128)S(1)}) custom-call(f32[1280,128]{1,0:T(8,128)S(1)} %bitcast.27), custom_call_target="tpu_custom_call" | custom-call | tf_op jit(solution)/shard_map/pallas_call | solution.py:136
  38.2 0.1 copy.25
  38.4 0.1 copy.34
  38.4 0.1 broadcast_in_dim.10
  38.5 0.1 copy.27
  38.5 0.1 broadcast_in_dim.11
  38.6 0.1 copy.28
  38.8 0.4 copy.30
  39.3 22.6 %all_to_all.11 = bf16[128,2,768]{2,1,0:T(2,128)(2,1)S(1)} all-to-all(bf16[128,2,768]{2,1,0:T(2,128)(2,1)S(1)} %copy.30), channel_id=1, replica_groups=mesh['context'=32,'tensor'=4,'dp'=4] {'context','dp'}, dimensions={0} | all-to-all | bytes 786432 | tf_op jit(solution)/shard_map/all_to_all | solution.py:171
  61.9 0.1 reshape.37
  62.1 0.8 %copy.32 = f32[256,256]{1,0:T(8,128)} copy(f32[256,256]{0,1:T(8,128)S(1)} %add_bitcast_fusion) | data formatting | bytes 524288
  63.0 0.8 %copy.31 = bf16[1,256,256]{2,1,0:T(8,128)(2,1)} copy(bf16[1,256,256]{1,2,0:T(8,128)(2,1)S(1)} %slice_bitcast_fusion) | data formatting | bytes 262144
  (6 shorter events, 0.1 us)
Async XLA Ops:
  0.6 0.9 %copy-start = (bf16[256,256]{1,0:T(8,128)(2,1)S(1)}, bf16[256,256]{1,0:T(8,128)(2,1)}, u32[]{:S(2)}) copy-start(bf16[256,256]{1,0:T(8,128)(2,1)} %param.5) | copy-start | bytes 393220
  0.6 1.0 %copy-start.1 = (bf16[1,256,256]{2,1,0:T(8,128)(2,1)S(1)}, bf16[1,256,256]{2,1,0:T(8,128)(2,1)}, u32[]{:S(2)}) copy-start(bf16[1,256,256]{2,1,0:T(8,128)(2,1)} %param.4) | copy-start | bytes 393220

commit v2 on v0

v2 whole, which is shorter than its diff:
```python
import functools
import jax
import jax.numpy as jnp
from jax import lax
from jax.experimental import pallas as pl
from jax.experimental.pallas import tpu as pltpu
from jax.sharding import PartitionSpec as P

F32 = jnp.float32
BF16 = jnp.bfloat16


def nt_dot(left, right):
    return lax.dot_general(left, right, (((1,), (1,)), ((), ())), preferred_element_type=F32)


def spread_row(ref, row, lane):
    return ref[pl.ds(2 * lane + row, 8, stride=0), :]


def lag_pieces(rows, out_ref):
    sub = lax.broadcasted_iota(jnp.int32, (8, 128), 0)
    lane = lax.broadcasted_iota(jnp.int32, (8, 128), 1)
    masks = [lane < sub + 8 * s for s in range(2)]
    before = [jnp.zeros((8, 128), F32) for _ in range(2)]
    for d in range(32):
        low, high = rows(d)
        pieces = []
        for s in range(2):
            low_turned = pltpu.roll(low, 8 * s, 1, stride=1, stride_axis=0)
            high_turned = pltpu.roll(high, 8 * s, 1, stride=1, stride_axis=0)
            pieces.append(
                jnp.concatenate(
                    [
                        jnp.where(masks[s], before[s], low_turned),
                        jnp.where(masks[s], low_turned, high_turned),
                    ],
                    axis=1,
                )
            )
            before[s] = high_turned
        out_ref[16 * d : 16 * d + 16, :] = jnp.concatenate(pieces, axis=0).astype(BF16)
        yield


def window_pieces(rows, out_ref, b):
    sub = lax.broadcasted_iota(jnp.int32, (8, 128), 0)
    lane = lax.broadcasted_iota(jnp.int32, (8, 128), 1)
    inside = lane < 16 + 16 * sub

    def turned(a):
        if a == 32:
            return [jnp.zeros((8, 128), F32)] * 2
        return [pltpu.roll(half, 16, 1, stride=16, stride_axis=0) for half in rows(a)]

    here = turned(0)
    first = jnp.where(inside, here[0], here[1])
    for a in range(32):
        after = turned(a + 1)
        second = jnp.where(inside, here[1], after[0])
        third = jnp.where(inside, after[0], after[1])
        block = jnp.concatenate(
            [
                jnp.concatenate([first, second], axis=1),
                jnp.concatenate([second, third], axis=1),
            ],
            axis=0,
        )
        out_ref[a, b] = block.astype(BF16)
        here, first = after, third
        yield


def product_pieces(left, lag_ref, total_ref, size, fresh):
    for q in range(2):
        part = nt_dot(left(16 * q), lag_ref[256 * q : 256 * q + 256, :])
        count = (32 - 16 * q) * size
        if fresh and q == 0:
            total_ref[0:count, :] = part[:, 0:128]
        else:
            total_ref[0:count, :] += part[:, 0:128]
        total_ref[0 : count - 8 * size, :] += part[8 * size :, 128:256]
        yield


def finish_pieces(total_ref, flat_ref, size, store):
    sub = lax.broadcasted_iota(jnp.int32, (8, 128), 0)
    lane = lax.broadcasted_iota(jnp.int32, (8, 128), 1)
    group = lane // 16
    keep = group == 7 - sub
    odd = [lax.rem(group // step, 2) == 1 for step in (1, 2, 4)]
    for rest in range(0, size, 8):

        def at(a):
            return total_ref[a * size + rest : a * size + rest + 8, :]

        ones, twos = {}, {}

        def one(a):
            if a not in ones:
                ones[a] = jnp.where(odd[0], at(a + 1), at(a))
            return ones[a]

        def two(a):
            if a not in twos:
                twos[a] = jnp.where(odd[1], one(a + 2), one(a))
            return twos[a]

        for a in range(32):
            row = a * size + rest
            flat_ref[row : row + 8, :] = jnp.where(odd[2], two(a + 4), two(a))
            if a % 8 == 7:
                yield
    keep_all = lax.broadcasted_iota(jnp.int32, (256, 128), 1) // 16 == 7 - lax.rem(
        lax.broadcasted_iota(jnp.int32, (256, 128), 0), 8
    )
    for turn in (64, 32, 16):
        for at in range(0, 32 * size, 256):
            mixed = flat_ref[at : at + 256, :]
            mixed = mixed + pltpu.roll(mixed, turn, 1)
            flat_ref[at : at + 256, :] = jnp.where(keep_all, mixed, 0.0) if turn == 16 else mixed
            yield
    for half in range(2):
        count = 2 * size
        store(
            half,
            sum(flat_ref[pl.ds(8 * half + i, count, stride=16), :] for i in range(8)),
        )
    yield


def interleave(*streams):
    done = [0] * len(streams)
    total = max(count for _, count in streams)
    for tick in range(1, total + 1):
        for at, (stream, count) in enumerate(streams):
            while done[at] * total < tick * count:
                next(stream)
                done[at] += 1
    for stream, _ in streams:
        for _ in stream:
            pass


def conv_kernel(r_ref, dx_ref, dh_ref, *scratch):
    window = scratch[0:2]
    lag_f = scratch[2:4]
    lag_x = scratch[4:8]
    total_dx = scratch[8:10]
    total_dh = scratch[10:12]
    flat_dx, flat_dh = scratch[12:14]

    def rows_of(part, shift):
        def rows(d):
            row = 8 * d + shift
            return (spread_row(r_ref, row, 128 * part), spread_row(r_ref, row, 128 * part + 128))

        return rows

    def filter_rows(c):
        def rows(d):
            return (spread_row(r_ref, 8 * d + c, 512), spread_row(r_ref, 8 * d + 4 + c, 512))

        return rows

    def signal_builds(c):
        builds = [(lag_pieces(filter_rows(c), lag_f[c]), 32)]
        for b in range(4):
            builds.append((window_pieces(rows_of(0, 2 * b + c), window[c], b), 32))
        return builds

    def lag_builds(c):
        return [(lag_pieces(rows_of(2, 2 * b + c), lag_x[b]), 32) for b in range(4)]

    def dx_products(c):
        def left(first):
            return window[c][first:].reshape((32 - first) * 64, 256)

        return (product_pieces(left, lag_f[c], total_dx[c], 64, True), 2)

    def dh_products(c):
        def chain():
            for b in range(4):

                def left(first):
                    return window[c][first:, b].reshape((32 - first) * 16, 256)

                yield from product_pieces(left, lag_x[b], total_dh[c], 16, b == 0)

        return (chain(), 8)

    def dx_finish(c):
        def store(half, rows):
            dx_ref[pl.ds(256 * half + c, 128, stride=2), :] = rows

        return (finish_pieces(total_dx[c], flat_dx, 64, store), 57)

    def dh_finish(c):
        def store(half, rows):
            dh_ref[pl.ds(64 * half + c, 32, stride=2), :] = rows

        return (finish_pieces(total_dh[c], flat_dh, 16, store), 15)

    for c in range(2):
        total_dx[c][2048:, :] = jnp.zeros((448, 128), F32)
        total_dh[c][512:, :] = jnp.zeros((112, 128), F32)
    interleave(*signal_builds(0))
    interleave(dx_products(0), *lag_builds(0))
    interleave(dh_products(0), *signal_builds(1), dx_finish(0))
    interleave(dx_products(1), *lag_builds(1), dh_finish(0))
    interleave(dh_products(1), dx_finish(1))
    interleave(dh_finish(1))


def conv_call(r):
    vmem = pl.BlockSpec(memory_space=pltpu.VMEM)
    return pl.pallas_call(
        conv_kernel,
        out_shape=(
            jax.ShapeDtypeStruct((512, 128), F32),
            jax.ShapeDtypeStruct((128, 128), F32),
        ),
        in_specs=[vmem],
        out_specs=(vmem, vmem),
        scratch_shapes=[pltpu.VMEM((32, 4, 16, 256), BF16)] * 2
        + [pltpu.VMEM((512, 256), BF16)] * 6
        + [pltpu.VMEM((2496, 128), F32)] * 2
        + [pltpu.VMEM((624, 128), F32)] * 2
        + [pltpu.VMEM((2048, 128), F32), pltpu.VMEM((512, 128), F32)],
        compiler_params=pltpu.CompilerParams(vmem_limit_bytes=24 * 1024 * 1024),
    )(r)


def body(grad_out, inputs, filt):
    turn = lax.axis_index("dp")
    wide = grad_out.shape[2]
    filter_turned = filt.T
    piece = lax.dynamic_slice(filter_turned, (0, 128 * (turn // 2)), (wide, 128))
    packed = jnp.concatenate([grad_out[0].T, inputs[0].T, piece], axis=1).reshape(128, 2, 640)
    arrived = lax.all_to_all(packed, ("context", "dp"), 0, 0, tiled=True)
    lanes = arrived.astype(F32).reshape(256, 5, 128).transpose(1, 0, 2).reshape(1280, 128)
    dx, dh = conv_call(lanes)
    dx = dx.reshape(2, 128, 2, 128).transpose(1, 2, 0, 3).reshape(128, 2, 256)
    dh = dh.reshape(2, 32, 2, 128).transpose(1, 2, 0, 3).reshape(32, 1, 2, 256)
    dh = jnp.broadcast_to(dh, (32, 4, 2, 256)).reshape(128, 2, 256)
    upper = lax.reduce_precision(dh, 8, 7)
    lower = (dh - upper).astype(BF16)
    outgoing = jnp.concatenate([dx.astype(BF16), upper.astype(BF16), lower], axis=2)
    returned = lax.all_to_all(outgoing, ("context", "dp"), 0, 0, tiled=True).reshape(256, 768)
    input_grad = returned[:, 0:256].T
    filter_grad = returned[:, 256:512].astype(F32) + returned[:, 512:768].astype(F32)
    return input_grad[None], filter_grad.T


def solution(mesh):
    return jax.shard_map(
        body,
        mesh=mesh,
        in_specs=(
            P("dp", "context", "tensor"),
            P("dp", "context", "tensor"),
            P("context", "tensor"),
        ),
        out_specs=(P("dp", "context", "tensor"), P("context", "tensor")),
        check_vma=False,
    )
```

time: 68.9 us -> 62.3 us (0.904)
  Pallas kernels: 7.94 us -> 3.94 us
  local copies, waits for them, and re-layouts: 5.8 us -> 4.27 us
  other arithmetic: 1.99 us -> 1.04 us
    pallas_call x1, Pallas kernels: 7.94 us -> 3.94 us  [conv_call(): pl.pallas_call(conv_kernel, out_shape=(jax.ShapeDtypeStruct((512, 128), F...]
    convert_element_type x1, other arithmetic: 0.96 us -> 0.02 us  [body(): dx.astype(BF16)]
    reshape x2, local copies, waits for them, and re-layouts: 1.14 us -> 0.31 us  [body(): arrived.astype(F32).reshape(256, 5, 128).transpose(1, 0, 2)]
    unnamed x8 -> x6, local copies, waits for them, and re-layouts: 3.23 us -> 2.53 us
where the time goes in v2:
time: 62.3 us; the launch traced here: 61.4 us
  blocking collectives  51.4 us (83%)
  local copies, waits for them, and re-layouts  4.27 us (7%)
  Pallas kernels  3.94 us (6%)
  other arithmetic  1.04 us (2%)
  between operations  0.79 us (1%)
    all_to_all x1, blocking collectives, body(): arrived = lax.all_to_all(packed, ('context', 'dp'), 0, 0, tiled=True)  28.8 us
    all_to_all x1, blocking collectives, body(): lax.all_to_all(outgoing, ('context', 'dp'), 0, 0, tiled=True)  22.6 us
    pallas_call x1, Pallas kernels, conv_call(): pl.pallas_call(conv_kernel, out_shape=(jax.ShapeDtypeStruct((512, 128), F...  3.94 us
    unnamed x6, local copies, waits for them, and re-layouts  2.53 us

profile of v2, /device:TPU:1, one launch (start us, length us, event | category | flops | bytes accessed | tf_op | source)
XLA Modules:
  0.0 61.4 jit_solution(1597451558547913446)
XLA Ops:
  0.6 0.0 copy-start
  0.6 0.0 copy-start.1
  0.7 0.9 %copy-done = bf16[256,256]{1,0:T(8,128)(2,1)S(1)} copy-done((bf16[256,256]{1,0:T(8,128)(2,1)S(1)}, bf16[256,256]{1,0:T(8,128)(2,1)}, u32[]{:S(2)}) %copy-start) | copy-done | bytes 131096
  1.5 0.1 copy-done.1
  1.6 0.9 %pad_maximum_fusion.1 = bf16[256,640]{0,1:T(8,128)(2,1)S(1)} fusion(bf16[256,128]{0,1:T(8,128)(2,1)S(1)} %dynamic-slice_bitcast_fusion, bf16[256,256]{0,1:T(8,128)(2,1)S(1)} %bitcast.34, bf16[256,256]{0,1:T(8,128)(2,1)} %bitcast.35), kind=kLoop, calls=%fused_computation.3 | loop fusion | flops 983040 | bytes 655360 | tf_op jit(solution)/shard_map/concatenate | solution.py:239
  2.5 0.2 copy.23
  2.7 0.1 reshape.31
  2.9 28.8 %all_to_all.10 = bf16[128,2,640]{2,1,0:T(2,128)(2,1)S(1)} all-to-all(bf16[128,2,640]{2,1,0:T(2,128)(2,1)S(1)} %reshape.31), channel_id=1, replica_groups=mesh['context'=32,'tensor'=4,'dp'=4] {'context','dp'}, dimensions={0} | all-to-all | bytes 655360 | tf_op jit(solution)/shard_map/all_to_all | solution.py:240
  31.7 0.2 reshape.42
  31.8 0.1 copy.24
  32.0 3.9 %shard_map.50 = (f32[512,128]{1,0:T(8,128)S(1)}, f32[128,128]{1,0:T(8,128)S(1)}) custom-call(f32[1280,128]{1,0:T(8,128)S(1)} %bitcast.27), custom_call_target="tpu_custom_call" | custom-call | tf_op jit(solution)/shard_map/pallas_call | solution.py:217
  36.0 0.1 copy.25
  36.1 0.1 copy.34
  36.1 0.1 broadcast_in_dim.10
  36.2 0.1 copy.27
  36.3 0.1 broadcast_in_dim.11
  36.3 0.1 copy.28
  36.6 0.4 copy.30
  37.0 22.6 %all_to_all.11 = bf16[128,2,768]{2,1,0:T(2,128)(2,1)S(1)} all-to-all(bf16[128,2,768]{2,1,0:T(2,128)(2,1)S(1)} %copy.30), channel_id=1, replica_groups=mesh['context'=32,'tensor'=4,'dp'=4] {'context','dp'}, dimensions={0} | all-to-all | bytes 786432 | tf_op jit(solution)/shard_map/all_to_all | solution.py:249
  59.6 0.1 reshape.37
  59.8 0.8 %copy.32 = f32[256,256]{1,0:T(8,128)} copy(f32[256,256]{0,1:T(8,128)S(1)} %add_bitcast_fusion) | data formatting | bytes 524288
  60.7 0.8 %copy.31 = bf16[1,256,256]{2,1,0:T(8,128)(2,1)} copy(bf16[1,256,256]{1,2,0:T(8,128)(2,1)S(1)} %slice_bitcast_fusion) | data formatting | bytes 262144
  (6 shorter events, 0.1 us)
Async XLA Ops:
  0.6 0.9 %copy-start = (bf16[256,256]{1,0:T(8,128)(2,1)S(1)}, bf16[256,256]{1,0:T(8,128)(2,1)}, u32[]{:S(2)}) copy-start(bf16[256,256]{1,0:T(8,128)(2,1)} %param.5) | copy-start | bytes 393220
  0.6 1.0 %copy-start.1 = (bf16[1,256,256]{2,1,0:T(8,128)(2,1)S(1)}, bf16[1,256,256]{2,1,0:T(8,128)(2,1)}, u32[]{:S(2)}) copy-start(bf16[1,256,256]{2,1,0:T(8,128)(2,1)} %param.4) | copy-start | bytes 393220

commit v3 on v2

--- a/solution.py
+++ b/solution.py
@@ -142,13 +142,14 @@
             pass
 
 
-def conv_kernel(r_ref, dx_ref, dh_ref, *scratch):
+def conv_kernel(r_ref, out_ref, *scratch):
     window = scratch[0:2]
     lag_f = scratch[2:4]
     lag_x = scratch[4:8]
     total_dx = scratch[8:10]
     total_dh = scratch[10:12]
     flat_dx, flat_dh = scratch[12:14]
+    dx_ref, dh_ref = scratch[14:16]
 
     def rows_of(part, shift):
         def rows(d):
@@ -197,7 +198,8 @@
 
     def dh_finish(c):
         def store(half, rows):
-            dh_ref[pl.ds(64 * half + c, 32, stride=2), :] = rows
+            for b in range(4):
+                dh_ref[pl.ds(256 * half + 2 * b + c, 32, stride=8), :] = rows
 
         return (finish_pieces(total_dh[c], flat_dh, 16, store), 15)
 
@@ -210,46 +212,72 @@
     interleave(dx_products(1), *lag_builds(1), dh_finish(0))
     interleave(dh_products(1), dx_finish(1))
     interleave(dh_finish(1))
+    for half in range(2):
+        rows, lanes = slice(256 * half, 256 * half + 256), slice(128 * half, 128 * half + 128)
+        out_ref[:, lanes] = dx_ref[rows, :].astype(BF16)
+        total = dh_ref[rows, :]
+        upper = total.astype(BF16)
+        out_ref[:, 256 + 128 * half : 384 + 128 * half] = upper
+        out_ref[:, 512 + 128 * half : 640 + 128 * half] = (total - upper.astype(F32)).astype(BF16)
 
 
 def conv_call(r):
     vmem = pl.BlockSpec(memory_space=pltpu.VMEM)
     return pl.pallas_call(
         conv_kernel,
-        out_shape=(
-            jax.ShapeDtypeStruct((512, 128), F32),
-            jax.ShapeDtypeStruct((128, 128), F32),
-        ),
+        out_shape=jax.ShapeDtypeStruct((256, 768), BF16),
         in_specs=[vmem],
-        out_specs=(vmem, vmem),
+        out_specs=vmem,
         scratch_shapes=[pltpu.VMEM((32, 4, 16, 256), BF16)] * 2
         + [pltpu.VMEM((512, 256), BF16)] * 6
         + [pltpu.VMEM((2496, 128), F32)] * 2
         + [pltpu.VMEM((624, 128), F32)] * 2
-        + [pltpu.VMEM((2048, 128), F32), pltpu.VMEM((512, 128), F32)],
+        + [pltpu.VMEM((2048, 128), F32), pltpu.VMEM((512, 128), F32)]
+        + [pltpu.VMEM((512, 128), F32)] * 2,
         compiler_params=pltpu.CompilerParams(vmem_limit_bytes=24 * 1024 * 1024),
     )(r)
 
 
+def unpack_kernel(r_ref, dx_hbm, dh_hbm, dx_ref, dh_ref, sems):
+    dh_ref[...] = (r_ref[:, 256:512].astype(F32) + r_ref[:, 512:768].astype(F32)).T
+    dh_copy = pltpu.make_async_copy(dh_ref, dh_hbm, sems.at[0])
+    dh_copy.start()
+    dx_ref[...] = r_ref[:, 0:256].T
+    dx_copy = pltpu.make_async_copy(dx_ref, dx_hbm.at[0], sems.at[1])
+    dx_copy.start()
+    dh_copy.wait()
+    dx_copy.wait()
+
+
+def unpack_call(returned):
+    hbm = pl.BlockSpec(memory_space=pl.ANY)
+    return pl.pallas_call(
+        unpack_kernel,
+        out_shape=(
+            jax.ShapeDtypeStruct((1, 256, 256), BF16),
+            jax.ShapeDtypeStruct((256, 256), F32),
+        ),
+        in_specs=[pl.BlockSpec(memory_space=pltpu.VMEM)],
+        out_specs=(hbm, hbm),
+        scratch_shapes=[
+            pltpu.VMEM((256, 256), BF16),
+            pltpu.VMEM((256, 256), F32),
+            pltpu.SemaphoreType.DMA((2,)),
+        ],
+        compiler_params=pltpu.CompilerParams(vmem_limit_bytes=4 * 1024 * 1024),
+    )(returned)
+
+
 def body(grad_out, inputs, filt):
     turn = lax.axis_index("dp")
-    wide = grad_out.shape[2]
-    filter_turned = filt.T
-    piece = lax.dynamic_slice(filter_turned, (0, 128 * (turn // 2)), (wide, 128))
-    packed = jnp.concatenate([grad_out[0].T, inputs[0].T, piece], axis=1).reshape(128, 2, 640)
+    both = lax.optimization_barrier(jnp.concatenate([grad_out[0], inputs[0]], axis=0))
+    piece = lax.dynamic_slice(filt, (128 * (turn // 2), 0), (128, 256))
+    packed = jnp.concatenate([both, piece], axis=0).T.reshape(128, 2, 640)
     arrived = lax.all_to_all(packed, ("context", "dp"), 0, 0, tiled=True)
     lanes = arrived.astype(F32).reshape(256, 5, 128).transpose(1, 0, 2).reshape(1280, 128)
-    dx, dh = conv_call(lanes)
-    dx = dx.reshape(2, 128, 2, 128).transpose(1, 2, 0, 3).reshape(128, 2, 256)
-    dh = dh.reshape(2, 32, 2, 128).transpose(1, 2, 0, 3).reshape(32, 1, 2, 256)
-    dh = jnp.broadcast_to(dh, (32, 4, 2, 256)).reshape(128, 2, 256)
-    upper = lax.reduce_precision(dh, 8, 7)
-    lower = (dh - upper).astype(BF16)
-    outgoing = jnp.concatenate([dx.astype(BF16), upper.astype(BF16), lower], axis=2)
-    returned = lax.all_to_all(outgoing, ("context", "dp"), 0, 0, tiled=True).reshape(256, 768)
-    input_grad = returned[:, 0:256].T
-    filter_grad = returned[:, 256:512].astype(F32) + returned[:, 512:768].astype(F32)
-    return input_grad[None], filter_grad.T
+    outgoing = conv_call(lanes).reshape(128, 2, 768)
+    returned = lax.all_to_all(outgoing, ("context", "dp"), 0, 0, tiled=True)
+    return unpack_call(returned.reshape(256, 768))
 
 
 def solution(mesh):

time: 62.3 us -> 59.9 us (0.961)
  local copies, waits for them, and re-layouts: 4.27 us -> 0.95 us
  Pallas kernels: 3.94 us -> 4.98 us
    unnamed x6 -> x2, local copies, waits for them, and re-layouts: 2.53 us -> 0.01 us
    pallas_call x1 -> x2, Pallas kernels: 3.94 us -> 4.98 us  [the longest x1 4.08 us: conv_call(): pl.pallas_call(conv_kernel, out_shape=jax.ShapeDtypeStruct((256, 768), BF...]
    concatenate x2 -> x0, local copies, waits for them, and re-layouts: 0.65 us -> none  [the longest x1 0.45 us: body(): jnp.concatenate([dx.astype(BF16), upper.astype(BF16), lower], axis=2)]
where the time goes in v3:
time: 59.9 us; the launch traced here: 59.1 us
  blocking collectives  51.4 us (86%)
  Pallas kernels  4.98 us (8%)
  other arithmetic  1.05 us (2%)
  local copies, waits for them, and re-layouts  0.95 us (2%)
  between operations  0.73 us (1%)
    all_to_all x1, blocking collectives, body(): arrived = lax.all_to_all(packed, ('context', 'dp'), 0, 0, tiled=True)  28.8 us
    all_to_all x1, blocking collectives, body(): returned = lax.all_to_all(outgoing, ('context', 'dp'), 0, 0, tiled=True)  22.6 us
    pallas_call x1, Pallas kernels, conv_call(): pl.pallas_call(conv_kernel, out_shape=jax.ShapeDtypeStruct((256, 768), BF...  4.08 us

profile of v3, /device:TPU:1, one launch (start us, length us, event | category | flops | bytes accessed | tf_op | source)
XLA Modules:
  0.0 59.1 jit_solution(7959333625186726745)
XLA Ops:
  0.6 0.0 copy-start
  0.7 1.0 %pad_maximum_fusion = bf16[512,256]{1,0:T(8,128)(2,1)S(1)} fusion(bf16[256,256]{1,0:T(8,128)(2,1)} %bitcast.8, bf16[256,256]{1,0:T(8,128)(2,1)} %bitcast.9), kind=kLoop, calls=%fused_computation.1 | loop fusion | flops 524288 | bytes 524288 | tf_op jit(solution)/shard_map/concatenate | solution.py:273
  1.7 0.0 copy-done
  1.8 0.2 copy.5
  2.0 0.1 reshape.22
  2.1 28.8 %all_to_all.10 = bf16[128,2,640]{2,1,0:T(2,128)(2,1)S(1)} all-to-all(bf16[128,2,640]{2,1,0:T(2,128)(2,1)S(1)} %reshape.22), channel_id=1, replica_groups=mesh['context'=32,'tensor'=4,'dp'=4] {'context','dp'}, dimensions={0} | all-to-all | bytes 655360 | tf_op jit(solution)/shard_map/all_to_all | solution.py:276
  30.9 0.2 reshape.32
  31.1 0.1 copy.6
  31.2 4.1 %shard_map.50 = bf16[256,768]{1,0:T(8,128)(2,1)S(1)} custom-call(f32[1280,128]{1,0:T(8,128)S(1)} %bitcast.6), custom_call_target="tpu_custom_call" | custom-call | tf_op jit(solution)/shard_map/pallas_call | solution.py:226
  35.3 0.1 reshape.26
  35.5 22.6 %all_to_all.11 = bf16[128,2,768]{2,1,0:T(2,128)(2,1)S(1)} all-to-all(bf16[128,2,768]{2,1,0:T(2,128)(2,1)S(1)} %reshape.26), channel_id=1, replica_groups=mesh['context'=32,'tensor'=4,'dp'=4] {'context','dp'}, dimensions={0} | all-to-all | bytes 786432 | tf_op jit(solution)/shard_map/all_to_all | solution.py:279
  58.1 0.1 reshape.27.r_ref
  58.2 0.9 %shard_map.51 = (bf16[1,256,256]{2,1,0:T(8,128)(2,1)}, f32[256,256]{1,0:T(8,128)}) custom-call(bf16[256,768]{1,0:T(8,128)(2,1)S(1)} %reshape.27.r_ref), custom_call_target="tpu_custom_call" | custom-call | tf_op jit(solution)/shard_map/pallas_call | solution.py:254
  (2 shorter events, 0.0 us)
Async XLA Ops:
  0.6 1.1 %copy-start = (bf16[256,256]{1,0:T(8,128)(2,1)S(1)}, bf16[256,256]{1,0:T(8,128)(2,1)}, u32[]{:S(2)}) copy-start(bf16[256,256]{1,0:T(8,128)(2,1)} %param.5) | copy-start | bytes 393220

commit v4 on v3

--- a/solution.py
+++ b/solution.py
@@ -1,4 +1,5 @@
-import functools
+import itertools
+
 import jax
 import jax.numpy as jnp
 from jax import lax
@@ -84,10 +85,7 @@
 
 
 def finish_pieces(total_ref, flat_ref, size, store):
-    sub = lax.broadcasted_iota(jnp.int32, (8, 128), 0)
-    lane = lax.broadcasted_iota(jnp.int32, (8, 128), 1)
-    group = lane // 16
-    keep = group == 7 - sub
+    group = lax.broadcasted_iota(jnp.int32, (8, 128), 1) // 16
     odd = [lax.rem(group // step, 2) == 1 for step in (1, 2, 4)]
     for rest in range(0, size, 8):
 
@@ -111,22 +109,21 @@
             flat_ref[row : row + 8, :] = jnp.where(odd[2], two(a + 4), two(a))
             if a % 8 == 7:
                 yield
-    keep_all = lax.broadcasted_iota(jnp.int32, (256, 128), 1) // 16 == 7 - lax.rem(
-        lax.broadcasted_iota(jnp.int32, (256, 128), 0), 8
-    )
-    for turn in (64, 32, 16):
-        for at in range(0, 32 * size, 256):
-            mixed = flat_ref[at : at + 256, :]
-            mixed = mixed + pltpu.roll(mixed, turn, 1)
-            flat_ref[at : at + 256, :] = jnp.where(keep_all, mixed, 0.0) if turn == 16 else mixed
+    count = min(2 * size, 32)
+    wide_group = lax.broadcasted_iota(jnp.int32, (count, 128), 1) // 16
+    wide_odd = [lax.rem(wide_group // step, 2) == 1 for step in (1, 2, 4)]
+    for half in range(2):
+        for first in range(0, 2 * size, count):
+            base = 16 * first + 8 * half + 7
+            terms = [flat_ref[pl.ds(base - (-k) % 8, count, stride=16), :] for k in range(8)]
+            for mask, step in zip(wide_odd, (1, 2, 4)):
+                terms = [jnp.where(mask, terms[(k - step) % 8], terms[k]) for k in range(8)]
+            for turn in (16, 32, 64):
+                terms = [
+                    terms[k] + pltpu.roll(terms[k + 1], 128 - turn, 1) for k in range(0, len(terms), 2)
+                ]
+            store(half, first, terms[0])
             yield
-    for half in range(2):
-        count = 2 * size
-        store(
-            half,
-            sum(flat_ref[pl.ds(8 * half + i, count, stride=16), :] for i in range(8)),
-        )
-    yield
 
 
 def interleave(*streams):
@@ -164,14 +161,14 @@
 
         return rows
 
-    def signal_builds(c):
-        builds = [(lag_pieces(filter_rows(c), lag_f[c]), 32)]
-        for b in range(4):
-            builds.append((window_pieces(rows_of(0, 2 * b + c), window[c], b), 32))
-        return builds
-
-    def lag_builds(c):
-        return [(lag_pieces(rows_of(2, 2 * b + c), lag_x[b]), 32) for b in range(4)]
+    def window_build(c, b):
+        return (window_pieces(rows_of(0, 2 * b + c), window[c], b), 32)
+
+    def lag_build(c, b):
+        return (lag_pieces(rows_of(2, 2 * b + c), lag_x[b]), 32)
+
+    def filter_build(c):
+        return (lag_pieces(filter_rows(c), lag_f[c]), 32)
 
     def dx_products(c):
         def left(first):
@@ -179,38 +176,38 @@
 
         return (product_pieces(left, lag_f[c], total_dx[c], 64, True), 2)
 
-    def dh_products(c):
-        def chain():
+    def dh_products(c, b):
+        def left(first):
+            return window[c][first:, b].reshape((32 - first) * 16, 256)
+
+        return (product_pieces(left, lag_x[b], total_dh[c], 16, b == 0), 2)
+
+    def dx_finish(c):
+        def store(half, first, rows):
+            dx_ref[pl.ds(256 * half + 2 * first + c, rows.shape[0], stride=2), :] = rows
+
+        return (finish_pieces(total_dx[c], flat_dx, 64, store), 40)
+
+    def dh_finish(c):
+        def store(half, first, rows):
             for b in range(4):
-
-                def left(first):
-                    return window[c][first:, b].reshape((32 - first) * 16, 256)
-
-                yield from product_pieces(left, lag_x[b], total_dh[c], 16, b == 0)
-
-        return (chain(), 8)
-
-    def dx_finish(c):
-        def store(half, rows):
-            dx_ref[pl.ds(256 * half + c, 128, stride=2), :] = rows
-
-        return (finish_pieces(total_dx[c], flat_dx, 64, store), 57)
-
-    def dh_finish(c):
-        def store(half, rows):
-            for b in range(4):
-                dh_ref[pl.ds(256 * half + 2 * b + c, 32, stride=8), :] = rows
-
-        return (finish_pieces(total_dh[c], flat_dh, 16, store), 15)
+                row = 256 * half + 8 * first + 2 * b + c
+                dh_ref[pl.ds(row, rows.shape[0], stride=8), :] = rows
+
+        return (finish_pieces(total_dh[c], flat_dh, 16, store), 10)
 
     for c in range(2):
         total_dx[c][2048:, :] = jnp.zeros((448, 128), F32)
         total_dh[c][512:, :] = jnp.zeros((112, 128), F32)
-    interleave(*signal_builds(0))
-    interleave(dx_products(0), *lag_builds(0))
-    interleave(dh_products(0), *signal_builds(1), dx_finish(0))
-    interleave(dx_products(1), *lag_builds(1), dh_finish(0))
-    interleave(dh_products(1), dx_finish(1))
+    interleave(window_build(0, 0), lag_build(0, 0))
+    for b in range(3):
+        interleave(dh_products(0, b), window_build(0, b + 1), lag_build(0, b + 1))
+    interleave(dh_products(0, 3), filter_build(0), window_build(1, 0))
+    later = [window_build(1, b) for b in range(1, 4)]
+    interleave(dx_products(0), filter_build(1), *later, dh_finish(0))
+    interleave(dx_products(1), *[lag_build(1, b) for b in range(4)], dx_finish(0))
+    last = [dh_products(1, b) for b in range(4)]
+    interleave((itertools.chain(*[pieces for pieces, _ in last]), 8), dx_finish(1))
     interleave(dh_finish(1))
     for half in range(2):
         rows, lanes = slice(256 * half, 256 * half + 256), slice(128 * half, 128 * half + 128)

time: 59.9 us -> 59.3 us (0.990)
  Pallas kernels: 4.98 us -> 4.31 us
    pallas_call x1, Pallas kernels: 4.08 us -> 3.41 us  [conv_call(): pl.pallas_call(conv_kernel, out_shape=jax.ShapeDtypeStruct((256, 768), BF...]
where the time goes in v4:
time: 59.3 us; the launch traced here: 58.4 us
  blocking collectives  51.4 us (87%)
  Pallas kernels  4.31 us (7%)
  other arithmetic  1.05 us (2%)
  local copies, waits for them, and re-layouts  0.95 us (2%)
  between operations  0.73 us (1%)
    all_to_all x1, blocking collectives, body(): arrived = lax.all_to_all(packed, ('context', 'dp'), 0, 0, tiled=True)  28.8 us
    all_to_all x1, blocking collectives, body(): returned = lax.all_to_all(outgoing, ('context', 'dp'), 0, 0, tiled=True)  22.6 us
    pallas_call x1, Pallas kernels, conv_call(): pl.pallas_call(conv_kernel, out_shape=jax.ShapeDtypeStruct((256, 768), BF...  3.41 us

profile of v4, /device:TPU:1, one launch (start us, length us, event | category | flops | bytes accessed | tf_op | source)
XLA Modules:
  0.0 58.4 jit_solution(7153145895126732009)
XLA Ops:
  0.6 0.0 copy-start
  0.7 1.0 %pad_maximum_fusion = bf16[512,256]{1,0:T(8,128)(2,1)S(1)} fusion(bf16[256,256]{1,0:T(8,128)(2,1)} %bitcast.8, bf16[256,256]{1,0:T(8,128)(2,1)} %bitcast.9), kind=kLoop, calls=%fused_computation.1 | loop fusion | flops 524288 | bytes 524288 | tf_op jit(solution)/shard_map/concatenate | solution.py:270
  1.7 0.0 copy-done
  1.8 0.2 copy.5
  2.0 0.1 reshape.22
  2.1 28.8 %all_to_all.10 = bf16[128,2,640]{2,1,0:T(2,128)(2,1)S(1)} all-to-all(bf16[128,2,640]{2,1,0:T(2,128)(2,1)S(1)} %reshape.22), channel_id=1, replica_groups=mesh['context'=32,'tensor'=4,'dp'=4] {'context','dp'}, dimensions={0} | all-to-all | bytes 655360 | tf_op jit(solution)/shard_map/all_to_all | solution.py:273
  30.9 0.2 reshape.32
  31.1 0.1 copy.6
  31.2 3.4 %shard_map.50 = bf16[256,768]{1,0:T(8,128)(2,1)S(1)} custom-call(f32[1280,128]{1,0:T(8,128)S(1)} %bitcast.6), custom_call_target="tpu_custom_call" | custom-call | tf_op jit(solution)/shard_map/pallas_call | solution.py:223
  34.6 0.1 reshape.26
  34.8 22.6 %all_to_all.11 = bf16[128,2,768]{2,1,0:T(2,128)(2,1)S(1)} all-to-all(bf16[128,2,768]{2,1,0:T(2,128)(2,1)S(1)} %reshape.26), channel_id=1, replica_groups=mesh['context'=32,'tensor'=4,'dp'=4] {'context','dp'}, dimensions={0} | all-to-all | bytes 786432 | tf_op jit(solution)/shard_map/all_to_all | solution.py:276
  57.4 0.1 reshape.27.r_ref
  57.5 0.9 %shard_map.51 = (bf16[1,256,256]{2,1,0:T(8,128)(2,1)}, f32[256,256]{1,0:T(8,128)}) custom-call(bf16[256,768]{1,0:T(8,128)(2,1)S(1)} %reshape.27.r_ref), custom_call_target="tpu_custom_call" | custom-call | tf_op jit(solution)/shard_map/pallas_call | solution.py:251
  (2 shorter events, 0.0 us)
Async XLA Ops:
  0.6 1.1 %copy-start = (bf16[256,256]{1,0:T(8,128)(2,1)S(1)}, bf16[256,256]{1,0:T(8,128)(2,1)}, u32[]{:S(2)}) copy-start(bf16[256,256]{1,0:T(8,128)(2,1)} %param.5) | copy-start | bytes 393220

commit v5 on v4

--- a/solution.py
+++ b/solution.py
@@ -16,7 +16,7 @@
 
 
 def spread_row(ref, row, lane):
-    return ref[pl.ds(2 * lane + row, 8, stride=0), :]
+    return jnp.broadcast_to(ref[row, lane // 128 : lane // 128 + 1, :], (8, 128))
 
 
 def lag_pieces(rows, out_ref):
@@ -109,13 +109,13 @@
             flat_ref[row : row + 8, :] = jnp.where(odd[2], two(a + 4), two(a))
             if a % 8 == 7:
                 yield
-    count = min(2 * size, 32)
+    count, step_rows = 32, size
     wide_group = lax.broadcasted_iota(jnp.int32, (count, 128), 1) // 16
     wide_odd = [lax.rem(wide_group // step, 2) == 1 for step in (1, 2, 4)]
     for half in range(2):
-        for first in range(0, 2 * size, count):
+        for first in range(size // 16):
             base = 16 * first + 8 * half + 7
-            terms = [flat_ref[pl.ds(base - (-k) % 8, count, stride=16), :] for k in range(8)]
+            terms = [flat_ref[pl.ds(base - (-k) % 8, count, stride=step_rows), :] for k in range(8)]
             for mask, step in zip(wide_odd, (1, 2, 4)):
                 terms = [jnp.where(mask, terms[(k - step) % 8], terms[k]) for k in range(8)]
             for turn in (16, 32, 64):
@@ -150,22 +150,22 @@
 
     def rows_of(part, shift):
         def rows(d):
-            row = 8 * d + shift
+            row = 2 * d + shift
             return (spread_row(r_ref, row, 128 * part), spread_row(r_ref, row, 128 * part + 128))
 
         return rows
 
     def filter_rows(c):
         def rows(d):
-            return (spread_row(r_ref, 8 * d + c, 512), spread_row(r_ref, 8 * d + 4 + c, 512))
+            return (spread_row(r_ref, 2 * d + c, 512), spread_row(r_ref, 2 * d + 128 + c, 512))
 
         return rows
 
     def window_build(c, b):
-        return (window_pieces(rows_of(0, 2 * b + c), window[c], b), 32)
+        return (window_pieces(rows_of(0, 64 * b + c), window[c], b), 32)
 
     def lag_build(c, b):
-        return (lag_pieces(rows_of(2, 2 * b + c), lag_x[b]), 32)
+        return (lag_pieces(rows_of(2, 64 * b + c), lag_x[b]), 32)
 
     def filter_build(c):
         return (lag_pieces(filter_rows(c), lag_f[c]), 32)
@@ -184,15 +184,14 @@
 
     def dx_finish(c):
         def store(half, first, rows):
-            dx_ref[pl.ds(256 * half + 2 * first + c, rows.shape[0], stride=2), :] = rows
+            dx_ref[pl.ds(256 * half + 64 * first + c, 32, stride=2), :] = rows
 
         return (finish_pieces(total_dx[c], flat_dx, 64, store), 40)
 
     def dh_finish(c):
         def store(half, first, rows):
             for b in range(4):
-                row = 256 * half + 8 * first + 2 * b + c
-                dh_ref[pl.ds(row, rows.shape[0], stride=8), :] = rows
+                dh_ref[pl.ds(256 * half + 64 * b + c, 32, stride=2), :] = rows
 
         return (finish_pieces(total_dh[c], flat_dh, 16, store), 10)
 
@@ -270,10 +269,10 @@
     both = lax.optimization_barrier(jnp.concatenate([grad_out[0], inputs[0]], axis=0))
     piece = lax.dynamic_slice(filt, (128 * (turn // 2), 0), (128, 256))
     packed = jnp.concatenate([both, piece], axis=0).T.reshape(128, 2, 640)
-    arrived = lax.all_to_all(packed, ("context", "dp"), 0, 0, tiled=True)
-    lanes = arrived.astype(F32).reshape(256, 5, 128).transpose(1, 0, 2).reshape(1280, 128)
+    arrived = lax.all_to_all(packed, ("dp", "context"), 0, 0, tiled=True)
+    lanes = arrived.astype(F32).reshape(256, 5, 128)
     outgoing = conv_call(lanes).reshape(128, 2, 768)
-    returned = lax.all_to_all(outgoing, ("context", "dp"), 0, 0, tiled=True)
+    returned = lax.all_to_all(outgoing, ("dp", "context"), 0, 0, tiled=True)
     return unpack_call(returned.reshape(256, 768))
 
 

time: 59.3 us -> 58.8 us (level); the launches traced: 58.4 us -> 58.6 us
  no operation moved by 1% of the time
where the time goes in v5:
time: 58.8 us; the launch traced here: 58.6 us
  blocking collectives  51.2 us (87%)
  Pallas kernels  4.87 us (8%)
  other arithmetic  1.05 us (2%)
  local copies, waits for them, and re-layouts  0.82 us (1%)
  between operations  0.72 us (1%)
    all_to_all x1, blocking collectives, body(): arrived = lax.all_to_all(packed, ('dp', 'context'), 0, 0, tiled=True)  29.3 us
    all_to_all x1, blocking collectives, body(): returned = lax.all_to_all(outgoing, ('dp', 'context'), 0, 0, tiled=True)  21.9 us
    pallas_call x1, Pallas kernels, conv_call(): pl.pallas_call(conv_kernel, out_shape=jax.ShapeDtypeStruct((256, 768), BF...  3.98 us

profile of v5, /device:TPU:1, one launch (start us, length us, event | category | flops | bytes accessed | tf_op | source)
XLA Modules:
  0.0 58.6 jit_solution(7241437094479583980)
XLA Ops:
  0.6 0.0 copy-start
  0.7 1.0 %pad_maximum_fusion = bf16[512,256]{1,0:T(8,128)(2,1)S(1)} fusion(bf16[256,256]{1,0:T(8,128)(2,1)} %bitcast.4, bf16[256,256]{1,0:T(8,128)(2,1)} %bitcast.5), kind=kLoop, calls=%fused_computation.1 | loop fusion | flops 524288 | bytes 524288 | tf_op jit(solution)/shard_map/concatenate | solution.py:269
  1.7 0.0 copy-done
  1.8 0.2 copy.6
  2.0 0.1 reshape.18
  2.1 29.3 %all_to_all.10 = bf16[128,2,640]{2,1,0:T(2,128)(2,1)S(1)} all-to-all(bf16[128,2,640]{2,1,0:T(2,128)(2,1)S(1)} %reshape.18), channel_id=1, replica_groups=mesh['context'=32,'tensor'=4,'dp'=4] {'dp','context'}, dimensions={0} | all-to-all | bytes 655360 | tf_op jit(solution)/shard_map/all_to_all | solution.py:272
  31.4 0.2 reshape.24.r_ref
  31.5 4.0 %shard_map.50 = bf16[256,768]{1,0:T(8,128)(2,1)S(1)} custom-call(f32[256,5,128]{2,1,0:T(8,128)S(1)} %reshape.24.r_ref), custom_call_target="tpu_custom_call" | custom-call | tf_op jit(solution)/shard_map/pallas_call | solution.py:222
  35.5 0.1 reshape.21
  35.7 21.9 %all_to_all.11 = bf16[128,2,768]{2,1,0:T(2,128)(2,1)S(1)} all-to-all(bf16[128,2,768]{2,1,0:T(2,128)(2,1)S(1)} %reshape.21), channel_id=1, replica_groups=mesh['context'=32,'tensor'=4,'dp'=4] {'dp','context'}, dimensions={0} | all-to-all | bytes 786432 | tf_op jit(solution)/shard_map/all_to_all | solution.py:275
  57.6 0.1 reshape.22.r_ref
  57.7 0.9 %shard_map.51 = (bf16[1,256,256]{2,1,0:T(8,128)(2,1)}, f32[256,256]{1,0:T(8,128)}) custom-call(bf16[256,768]{1,0:T(8,128)(2,1)S(1)} %reshape.22.r_ref), custom_call_target="tpu_custom_call" | custom-call | tf_op jit(solution)/shard_map/pallas_call | solution.py:250
  (2 shorter events, 0.0 us)
Async XLA Ops:
  0.6 1.1 %copy-start = (bf16[256,256]{1,0:T(8,128)(2,1)S(1)}, bf16[256,256]{1,0:T(8,128)(2,1)}, u32[]{:S(2)}) copy-start(bf16[256,256]{1,0:T(8,128)(2,1)} %param.5) | copy-start | bytes 393220
